TPU v7x, 128 devices: a whole 4x4x4 slice. The times are simulated.
128 devices in a mesh: lon: 8 (over x, y_hi), lat: 16 (over y_lo, z, core).
Axes of the slice: x: 4, y: 4 (y_hi: 2, y_lo: 2; y = y_hi * 2 + y_lo), z: 4, core: 2. Of those that a mesh axis runs over, the one named last changes fastest.
Arguments:
- field: float32 [32, 768, 3072], P(None, 'lat', 'lon'), may hold values from -6 to 6
- vertical: float32 [32, 32], replicated, may hold values from -1.5 to 1.5, as said below
- rate: float32 [32, 768], P(None, 'lat'), may hold values from 3.2552085e-05 to 0.5
- lat_kernel: float32 [768, 768], replicated, may hold values from 0 to 1, as said below
Outputs:
- increment: float32 [32, 768, 3072], P(None, 'lat', 'lon')
Inputs may be any that keep to these rules, and one draw needn't show every extreme that they name: `vertical`: the identity plus independent terms of magnitude at most 0.5 times 4 / sqrt(32). `lat_kernel`: Non-negative weights.
All inputs are finite; a program needn't handle non-finite values.
Results may differ from a plain program's by a relative error of at most 0.00015.
Values sent between devices are 32-bit elements; how exact they have to be, the bound alone decides.
No kernel may reach another device: no remote copies, remote signals or barrier semaphores. Data moves between devices by JAX's collectives and lax.ppermute only.
A program may use at most 128 MiB of HBM per device.

v0:
```python
import functools

import jax
import jax.numpy as jnp
from jax import lax
from jax.experimental import pallas as pl
from jax.experimental.pallas import tpu as pltpu
from jax.sharding import PartitionSpec as P

LANES = 128
SUB = 8
MID = LANES // 2


def split(x):
    high = x.astype(jnp.bfloat16)
    return high, (x - high.astype(jnp.float32)).astype(jnp.bfloat16)


def dot(a, b):
    return jnp.dot(a, b, preferred_element_type=jnp.float32)


def dot3(a_high, a_low, b_high, b_low):
    return dot(a_high, b_high) + (dot(a_high, b_low) + dot(a_low, b_high))


def iota(shape, dim):
    return lax.broadcasted_iota(jnp.int32, shape, dim)


def log_decays(rate):
    decay = 1.0 - rate
    gap = decay - 1.0
    return jnp.log(decay) * (rate / -gap)


def columns(tile, levels):
    return jnp.concatenate([jnp.broadcast_to(tile[:, k : k + 1], (SUB, LANES)) for k in range(levels)], 0)


def filter_kernel(field_hbm, vertical_hbm, rate_hbm, out_ref, edge_ref, decay_ref, turned_ref, field_ref, vertical_ref, rate_ref, matrix_ref, sums_ref, edges_ref, sems):
    groups, levels, _, lons = field_ref.shape
    rows = levels * SUB
    lats = groups * SUB
    tiles = lons // LANES
    small = [
        pltpu.make_async_copy(rate_hbm, rate_ref, sems.at[groups]),
        pltpu.make_async_copy(vertical_hbm, vertical_ref, sems.at[groups + 1]),
    ]
    for copy in small:
        copy.start()
    copies = [pltpu.make_async_copy(field_hbm.at[:, pl.ds(g * SUB, SUB), :], field_ref.at[g], sems.at[g]) for g in range(groups)]
    for copy in copies:
        copy.start()
    spread = (iota((rows, levels), 0) // SUB == iota((rows, levels), 1)).astype(jnp.bfloat16)
    across = (iota((levels, rows), 1) // SUB == iota((levels, rows), 0)).astype(jnp.bfloat16)
    same = iota((rows, rows), 0) % SUB == iota((rows, rows), 1) % SUB
    source, target = iota((2 * LANES, 2 * LANES), 0) % LANES, iota((2 * LANES, 2 * LANES), 1)
    sums_ref[0] = ((source <= target) | (target >= LANES)).astype(jnp.bfloat16)
    sums_ref[1] = ((source > target) | (target >= LANES)).astype(jnp.bfloat16)
    edges_ref[...] = jnp.zeros_like(edges_ref)
    small[0].wait()
    filled = jnp.full((levels, MID - lats), 0.5, jnp.float32)
    rate = rate_ref[...]
    rate = jnp.concatenate([rate, filled, rate, filled], 1)
    rest = jnp.zeros((LANES - levels, LANES), jnp.float32)
    log_decay = log_decays(rate)
    decay_ref[...] = log_decay
    turned_ref[0] = jnp.concatenate([log_decay, rest], 0).T
    turned_ref[1] = jnp.concatenate([rate / (2.0 - rate), rest], 0).T
    small[1].wait()
    for i, piece in enumerate(split(vertical_ref[...])):
        tall = dot(spread, piece).astype(jnp.bfloat16)
        matrix_ref[i] = jnp.where(same, dot(tall, across), 0.0).astype(jnp.bfloat16)

    narrow = iota((SUB, LANES), 1)
    offset = (iota((rows, LANES), 1) - MID).astype(jnp.float32)
    for g in range(groups):
        if g % 3 == 0:
            for copy in copies[g : g + 3]:
                copy.wait()
        x_high, x_low = split(field_ref[g].reshape(rows, lons))
        mixed = dot3(matrix_ref[0], matrix_ref[1], x_high, x_low)
        here = slice(g * SUB, (g + 1) * SUB)
        log_decay, gain = columns(turned_ref[0, here], levels), columns(turned_ref[1, here], levels)
        falling, rising = jnp.exp(offset * log_decay), jnp.exp(-offset * log_decay)
        half = jnp.exp(MID * log_decay)

        def summed(scale, sums):
            pieces = [jnp.concatenate(split(mixed[:, c * LANES : (c + 1) * LANES] * scale), 1) for c in range(tiles)]
            both = dot(jnp.concatenate(pieces, 0), sums)
            return [both[c * rows : (c + 1) * rows, :LANES] for c in range(tiles)], [both[c * rows : (c + 1) * rows, LANES:] for c in range(tiles)]

        east, all_east = summed(rising * gain, sums_ref[0])
        west, all_west = summed(falling * gain, sums_ref[1])
        carry = 0.0
        for c in range(tiles):
            east[c] = east[c] + carry
            last = half * (all_east[c] + carry)
            carry = half * last
        carry = 0.0
        for c in range(tiles - 1, -1, -1):
            west[c] = west[c] + carry
            first = half * (all_west[c] + carry)
            carry = half * first
        for c in range(tiles):
            total = falling * east[c] + rising * west[c]
            out_ref[:, :, g * tiles + c] = total.reshape(levels // 2, 2, SUB, LANES)
        for value, base in ((last, 0), (first, MID)):
            edges = jnp.zeros((SUB, LANES), jnp.float32)
            for k in range(levels):
                edges = jnp.where(narrow == k, value[k * SUB : (k + 1) * SUB], edges)
            edges_ref[base + g * SUB : base + (g + 1) * SUB, :] = edges
    edge_ref[...] = jnp.broadcast_to(edges_ref[...].T[None, :levels], edge_ref.shape)


HBM = pl.BlockSpec(memory_space=pltpu.HBM)
VMEM = pl.BlockSpec(memory_space=pltpu.VMEM)


def filtered_blocks(ring, field, vertical, rate):
    levels, lats, lons = field.shape
    groups, rows, tiles = lats // SUB, levels * SUB, lons // LANES
    return pl.pallas_call(
        filter_kernel,
        in_specs=[HBM] * 3,
        out_specs=[VMEM] * 4,
        out_shape=[
            jax.ShapeDtypeStruct((levels // 2, 2, groups * tiles, SUB, LANES), jnp.float32),
            jax.ShapeDtypeStruct((ring, levels, LANES), jnp.float32),
            jax.ShapeDtypeStruct((levels, LANES), jnp.float32),
            jax.ShapeDtypeStruct((2, LANES, LANES), jnp.float32),
        ],
        scratch_shapes=[
            pltpu.VMEM((groups, levels, SUB, lons), jnp.float32),
            pltpu.VMEM(vertical.shape, jnp.float32),
            pltpu.VMEM(rate.shape, jnp.float32),
            pltpu.VMEM((2, rows, rows), jnp.bfloat16),
            pltpu.VMEM((2, 2 * LANES, 2 * LANES), jnp.bfloat16),
            pltpu.VMEM((LANES, LANES), jnp.float32),
            pltpu.SemaphoreType.DMA((groups + 2,)),
        ],
        compiler_params=pltpu.CompilerParams(vmem_limit_bytes=16 << 20),
        cost_estimate=pl.CostEstimate(flops=16 * 10**8, bytes_accessed=5 * 10**6, transcendentals=2 * 10**5),
        name="mix_filter",
    )(*[pltpu.with_memory_space_constraint(v, pltpu.HBM) for v in (field, vertical, rate)])


def add_states_kernel(width, place_ref, decay_ref, turned_ref, edge_ref, values_ref, out_ref, state_ref):
    ring, levels, _ = edge_ref.shape
    tiles = width // LANES
    groups = out_ref.shape[2] // tiles
    rows = levels * SUB
    log_decay = decay_ref[...]
    eastward = iota((levels, LANES), 1) < MID
    total = jnp.zeros((levels, LANES), jnp.float32)
    for device in range(ring):
        away = (place_ref[0] + ring - device) % ring
        blocks = jnp.where(eastward, (away + ring - 1) % ring, ring - 1 - away).astype(jnp.float32)
        total = total + edge_ref[device] * jnp.exp(blocks * (width * log_decay))
    total = total / (1.0 - jnp.exp((ring * width) * log_decay))
    state_ref[...] = jnp.concatenate([total, jnp.zeros((LANES - levels, LANES), jnp.float32)], 0).T
    lane = iota((rows, LANES), 1).astype(jnp.float32)
    for g in range(groups):
        log_decay = columns(turned_ref[0, g * SUB : (g + 1) * SUB], levels)
        hop = jnp.exp(float(LANES) * log_decay)
        wests = [columns(state_ref[g * SUB : (g + 1) * SUB], levels) * jnp.exp(log_decay * lane)]
        easts = [columns(state_ref[MID + g * SUB : MID + (g + 1) * SUB], levels) * jnp.exp(log_decay * (LANES - lane))]
        for _ in range(tiles - 1):
            wests.append(wests[-1] * hop)
            easts.append(easts[-1] * hop)
        for c in range(tiles):
            more = wests[c] + easts[tiles - 1 - c]
            out_ref[:, :, g * tiles + c] = values_ref[:, :, g * tiles + c] + more.reshape(levels // 2, 2, SUB, LANES)


def with_states(width, where, decay, turned, edges, values):
    return pl.pallas_call(
        functools.partial(add_states_kernel, width),
        in_specs=[pl.BlockSpec(memory_space=pltpu.SMEM)] + [VMEM] * 4,
        out_specs=VMEM,
        out_shape=jax.ShapeDtypeStruct(values.shape, values.dtype),
        scratch_shapes=[pltpu.VMEM((LANES, LANES), jnp.float32)],
        input_output_aliases={4: 0},
        compiler_params=pltpu.CompilerParams(vmem_limit_bytes=16 << 20),
        cost_estimate=pl.CostEstimate(flops=10**7, bytes_accessed=5 * 10**6, transcendentals=10**5),
        name="add_states",
    )(where, decay, turned, edges, values)


def convolve_kernel(values_ref, kernel_ref, out_ref, high_ref, low_ref):
    sources, parts, lats, lons = out_ref.shape
    tiles = lons // LANES
    groups = lats // SUB
    for part in range(parts):
        for source in range(sources):
            rows = slice(source * lats, (source + 1) * lats)
            for c in range(tiles):
                values = jnp.concatenate([values_ref[source, part, g * tiles + c] for g in range(groups)], 0)
                cols = slice((part * tiles + c) * LANES, (part * tiles + c + 1) * LANES)
                high_ref[rows, cols], low_ref[rows, cols] = split(values)
    group = 4
    for j in range(0, sources, group):
        k_high, k_low = split(kernel_ref[j * lats : (j + group) * lats])
        for part in range(parts):
            cols = slice(part * lons, (part + 1) * lons)
            result = dot3(k_high, k_low, high_ref[:, cols], low_ref[:, cols])
            out_ref[j : j + group, part] = result.reshape(group, lats, lons)


def convolved(values, lat_kernel, lats, lons):
    sources = values.shape[0]
    nlat = sources * lats
    return pl.pallas_call(
        convolve_kernel,
        in_specs=[VMEM] * 2,
        out_specs=VMEM,
        out_shape=jax.ShapeDtypeStruct((sources, 2, lats, lons), jnp.float32),
        scratch_shapes=[
            pltpu.VMEM((nlat, 2 * lons), jnp.bfloat16),
            pltpu.VMEM((nlat, 2 * lons), jnp.bfloat16),
        ],
        compiler_params=pltpu.CompilerParams(vmem_limit_bytes=16 << 20),
        cost_estimate=pl.CostEstimate(flops=28 * 10**8, bytes_accessed=8 * 10**6, transcendentals=0),
        name="convolve",
    )(values, lat_kernel)


def in_place(v):
    return pl.pallas_call(
        lambda v_ref, out_ref: None,
        in_specs=[HBM],
        out_specs=HBM,
        out_shape=jax.ShapeDtypeStruct(v.shape, v.dtype),
        input_output_aliases={0: 0},
        compiler_params=pltpu.CompilerParams(vmem_limit_bytes=1 << 20),
        name="in_place",
    )(pltpu.with_memory_space_constraint(v, pltpu.HBM))


def on_device(field, vertical, rate, lat_kernel):
    ring = lax.axis_size("lon")
    levels, lats, lons = field.shape
    where = lax.axis_index("lon").reshape(1)

    def exchanged(v, axis):
        return lax.all_to_all(v, axis, 0, 0, tiled=True)

    values, edges, decay, turned = filtered_blocks(ring, field, vertical, rate)
    where, edges = lax.optimization_barrier((where, edges))
    values = with_states(lons, where, decay, turned, exchanged(edges, "lon"), values)
    out = convolved(exchanged(values, "lat"), lat_kernel, lats, lons)
    return exchanged(out, "lat").reshape(levels, lats, lons)


def solution(mesh):
    return jax.shard_map(
        on_device,
        mesh=mesh,
        in_specs=(P(None, "lat", "lon"), P(), P(None, "lat"), P()),
        out_specs=P(None, "lat", "lon"),
        check_vma=False,
    )
```

profile of v0, /device:TPU:1, one launch (start us, length us, event | category | flops | bytes accessed | tf_op | source)
XLA Modules:
  0.0 96.5 jit_solution(17899518689508870791)
XLA Ops:
  0.0 5.0 %mix_filter.1 = (f32[16,2,18,8,128]{4,3,2,1,0:T(8,128)S(1)}, f32[8,32,128]{2,1,0:T(8,128)S(1)}, f32[32,128]{1,0:T(8,128)S(1)}, f32[2,128,128]{2,1,0:T(8,128)S(1)}) custom-call(f32[32,48,384]{2,1,0:T(8,128)} %field_hbm.1, f32[32,32]{1,0:T(8,128)} %vertical_hbm.1, f32[32,48]{1,0:T(8,128)} %rate_hbm.1), custom_call_target="tpu_custom_call" | custom-call | flops 1600000000 | bytes 5000000 | tf_op jit(solution)/shard_map/mix_filter/pallas_call | solution.py:125
  5.0 14.0 %all_to_all.15.edge_ref = f32[8,32,128]{2,1,0:T(8,128)S(1)} all-to-all(f32[8,32,128]{2,1,0:T(8,128)S(1)} %get-tuple-element.15), channel_id=1, replica_groups=mesh['lon'=8,'lat'=16] {'lon'}, dimensions={0} | all-to-all | bytes 262144 | tf_op jit(solution)/shard_map/all_to_all | solution.py:248
  19.0 1.9 %add_states.1 = f32[16,2,18,8,128]{4,3,2,1,0:T(8,128)S(1)} custom-call(s32[1]{0:T(128)} %bitcast.place_ref, f32[32,128]{1,0:T(8,128)S(1)} %get-tuple-element.13.decay_ref, f32[2,128,128]{2,1,0:T(8,128)S(1)} %get-tuple-element.14.turned_ref, f32[8,32,128]{2,1,0:T(8,128)S(1)} %all_to_all.15.edge_ref, ...), custom_call_target="tpu_custom_call", output_to_operand_aliasing={{}: (4, {})} | custom-call | flops 10000000 | bytes 5000000 | tf_op jit(solution)/shard_map/add_states/pallas_call | solution.py:179
  20.9 0.0 copy-start
  20.9 37.1 %all_to_all.16.values_ref = f32[16,2,18,8,128]{4,3,2,1,0:T(8,128)S(1)} all-to-all(f32[16,2,18,8,128]{4,3,2,1,0:T(8,128)S(1)} %add_states.1), channel_id=1, replica_groups=mesh['lon'=8,'lat'=16] {'lat'}, dimensions={0} | all-to-all | bytes 4718592 | tf_op jit(solution)/shard_map/all_to_all | solution.py:248
  58.0 0.0 copy-done
  58.0 4.0 %convolve.1 = f32[16,2,48,384]{3,2,1,0:T(8,128)S(1)} custom-call(f32[16,2,18,8,128]{4,3,2,1,0:T(8,128)S(1)} %all_to_all.16.values_ref, f32[768,768]{1,0:T(8,128)S(1)} %copy-done), custom_call_target="tpu_custom_call" | custom-call | flops 2800000000 | bytes 8000000 | tf_op jit(solution)/shard_map/convolve/pallas_call | solution.py:215
  62.0 33.1 %all_to_all.17 = f32[16,2,48,384]{3,2,1,0:T(8,128)S(1)} all-to-all(f32[16,2,48,384]{3,2,1,0:T(8,128)S(1)} %convolve.1), channel_id=1, replica_groups=mesh['lon'=8,'lat'=16] {'lat'}, dimensions={0} | all-to-all | bytes 4718592 | tf_op jit(solution)/shard_map/all_to_all | solution.py:248
  95.1 1.4 %copy.8 = f32[32,48,384]{2,1,0:T(8,128)} copy(f32[32,48,384]{2,1,0:T(8,128)S(1)} %bitcast.2) | data formatting | bytes 4718592
Async XLA Ops:
  20.9 37.1 %copy-start = (f32[768,768]{1,0:T(8,128)S(1)}, f32[768,768]{1,0:T(8,128)}, u32[]{:S(2)}) copy-start(f32[768,768]{1,0:T(8,128)} %kernel_ref.1) | copy-start | bytes 7077892
where the time goes:
time: 96.8 us; the launch traced here: 96.5 us
  blocking collectives  84.3 us (87%)
  Pallas kernels  10.8 us (11%)
  local copies, waits for them, and re-layouts  1.41 us (1%)
    all_to_all x3, blocking collectives, exchanged(): return lax.all_to_all(v, axis, 0, 0, tiled=True)  84.3 us
    pallas_call x1, Pallas kernels, filtered_blocks(): pl.pallas_call(filter_kernel, in_specs=[HBM] * 3, out_specs=[VMEM] * 4, o...  5 us
    pallas_call x1, Pallas kernels, convolved(): pl.pallas_call(convolve_kernel, in_specs=[VMEM] * 2, out_specs=VMEM, out_...  3.97 us

commit v1 on v0

v1 whole, which is shorter than its diff:
```python
import functools

import jax
import jax.numpy as jnp
from jax import lax
from jax.experimental import pallas as pl
from jax.experimental.pallas import tpu as pltpu
from jax.sharding import PartitionSpec as P

LANES = 128
SUB = 8
MID = LANES // 2


def split(x):
    high = x.astype(jnp.bfloat16)
    return high, (x - high.astype(jnp.float32)).astype(jnp.bfloat16)


def dot(a, b):
    return jnp.dot(a, b, preferred_element_type=jnp.float32)


def dot3(a_high, a_low, b_high, b_low):
    return dot(a_high, b_high) + (dot(a_high, b_low) + dot(a_low, b_high))


def iota(shape, dim):
    return lax.broadcasted_iota(jnp.int32, shape, dim)


def log_decays(rate):
    decay = 1.0 - rate
    gap = decay - 1.0
    return jnp.log(decay) * (rate / -gap)


def columns(tile, levels):
    return jnp.concatenate([jnp.broadcast_to(tile[:, k : k + 1], (SUB, LANES)) for k in range(levels)], 0)


def mix_kernel(batch, field_hbm, vertical_hbm, rate_hbm, mixed_ref, edge_ref, decay_ref, turned_ref, field_ref, vertical_ref, rate_ref, matrix_ref, edges_ref, sems):
    groups, rows, lons = mixed_ref.shape
    levels = rows // SUB
    lats = groups * SUB
    tiles = lons // LANES
    small = [
        pltpu.make_async_copy(rate_hbm, rate_ref, sems.at[groups]),
        pltpu.make_async_copy(vertical_hbm, vertical_ref, sems.at[groups + 1]),
    ]
    for copy in small:
        copy.start()
    copies = [pltpu.make_async_copy(field_hbm.at[:, pl.ds(g * SUB, SUB), :], field_ref.at[g], sems.at[g]) for g in range(groups)]
    for copy in copies:
        copy.start()
    spread = (iota((rows, levels), 0) // SUB == iota((rows, levels), 1)).astype(jnp.bfloat16)
    across = (iota((levels, rows), 1) // SUB == iota((levels, rows), 0)).astype(jnp.bfloat16)
    same = iota((rows, rows), 0) % SUB == iota((rows, rows), 1) % SUB
    ones = jnp.ones((2 * LANES, LANES), jnp.bfloat16)
    edges_ref[...] = jnp.zeros_like(edges_ref)
    small[0].wait()
    filled = jnp.full((levels, MID - lats), 0.5, jnp.float32)
    rate = rate_ref[...]
    rate = jnp.concatenate([rate, filled, rate, filled], 1)
    rest = jnp.zeros((LANES - levels, LANES), jnp.float32)
    log_decay = log_decays(rate)
    decay_ref[...] = log_decay
    turned_ref[0] = jnp.concatenate([log_decay, rest], 0).T
    turned_ref[1] = jnp.concatenate([rate / (2.0 - rate), rest], 0).T
    small[1].wait()
    for i, piece in enumerate(split(vertical_ref[...])):
        tall = dot(spread, piece).astype(jnp.bfloat16)
        matrix_ref[i] = jnp.where(same, dot(tall, across), 0.0).astype(jnp.bfloat16)

    lane = iota((rows, LANES), 1).astype(jnp.float32)
    narrow = iota((SUB, LANES), 1)
    for first_group in range(0, groups, batch):
        batched = range(first_group, first_group + batch)
        for g in batched:
            copies[g].wait()
        x_high, x_low = split(jnp.concatenate([field_ref[g].reshape(rows, lons) for g in batched], 1))
        mixed_batch = dot3(matrix_ref[0], matrix_ref[1], x_high, x_low)
        for at, g in enumerate(batched):
            mixed = mixed_batch[:, at * lons : (at + 1) * lons]
            mixed_ref[g] = mixed
            value = [mixed[:, c * LANES : (c + 1) * LANES] for c in range(tiles)]
            here = slice(g * SUB, (g + 1) * SUB)
            log_decay = columns(turned_ref[0, here], levels)
            hop = jnp.exp(float(LANES) * log_decay)
            last, first = value[0], value[-1]
            for c in range(1, tiles):
                last = last * hop + value[c]
                first = first * hop + value[tiles - 1 - c]
            last = last * jnp.exp((LANES - lane) * log_decay)
            first = first * jnp.exp(lane * log_decay)
            for weighted, base in ((last, 0), (first, MID)):
                total = dot(jnp.concatenate(split(weighted), 1), ones)
                edges = jnp.zeros((SUB, LANES), jnp.float32)
                for k in range(levels):
                    edges = jnp.where(narrow == k, total[k * SUB : (k + 1) * SUB], edges)
                edges_ref[base + g * SUB : base + (g + 1) * SUB, :] = edges * turned_ref[1, here]
    edge_ref[...] = jnp.broadcast_to(edges_ref[...].T[None, :levels], edge_ref.shape)


HBM = pl.BlockSpec(memory_space=pltpu.HBM)
VMEM = pl.BlockSpec(memory_space=pltpu.VMEM)


def mixed_levels(ring, field, vertical, rate):
    levels, lats, lons = field.shape
    groups, rows = lats // SUB, levels * SUB
    return pl.pallas_call(
        functools.partial(mix_kernel, 2 if groups % 2 == 0 else 1),
        in_specs=[HBM] * 3,
        out_specs=[VMEM] * 4,
        out_shape=[
            jax.ShapeDtypeStruct((groups, rows, lons), jnp.float32),
            jax.ShapeDtypeStruct((ring, levels, LANES), jnp.float32),
            jax.ShapeDtypeStruct((levels, LANES), jnp.float32),
            jax.ShapeDtypeStruct((2, LANES, LANES), jnp.float32),
        ],
        scratch_shapes=[
            pltpu.VMEM((groups, levels, SUB, lons), jnp.float32),
            pltpu.VMEM(vertical.shape, jnp.float32),
            pltpu.VMEM(rate.shape, jnp.float32),
            pltpu.VMEM((2, rows, rows), jnp.bfloat16),
            pltpu.VMEM((LANES, LANES), jnp.float32),
            pltpu.SemaphoreType.DMA((groups + 2,)),
        ],
        compiler_params=pltpu.CompilerParams(vmem_limit_bytes=16 << 20),
        cost_estimate=pl.CostEstimate(flops=8 * 10**8, bytes_accessed=5 * 10**6, transcendentals=2 * 10**5),
        name="mix",
    )(*[pltpu.with_memory_space_constraint(v, pltpu.HBM) for v in (field, vertical, rate)])


def filter_kernel(place_ref, decay_ref, turned_ref, edge_ref, mixed_ref, out_ref, state_ref):
    groups, rows, lons = mixed_ref.shape
    ring, levels, _ = edge_ref.shape
    tiles = lons // LANES
    log_decay = decay_ref[...]
    eastward = iota((levels, LANES), 1) < MID
    total = jnp.zeros((levels, LANES), jnp.float32)
    for device in range(ring):
        away = (place_ref[0] + ring - device) % ring
        blocks = jnp.where(eastward, (away + ring - 1) % ring, ring - 1 - away).astype(jnp.float32)
        total = total + edge_ref[device] * jnp.exp(blocks * (lons * log_decay))
    total = total / (1.0 - jnp.exp((ring * lons) * log_decay))
    state_ref[...] = jnp.concatenate([total, jnp.zeros((LANES - levels, LANES), jnp.float32)], 0).T
    source, target = iota((2 * LANES, 2 * LANES), 0) % LANES, iota((2 * LANES, 2 * LANES), 1)
    sums_east = ((source <= target) | (target >= LANES)).astype(jnp.bfloat16)
    sums_west = ((source > target) | (target >= LANES)).astype(jnp.bfloat16)
    offset = (iota((rows, LANES), 1) - MID).astype(jnp.float32)
    for g in range(groups):
        here = slice(g * SUB, (g + 1) * SUB)
        log_decay, gain = columns(turned_ref[0, here], levels), columns(turned_ref[1, here], levels)
        falling, rising = jnp.exp(offset * log_decay), jnp.exp(-offset * log_decay)
        half = jnp.exp(MID * log_decay)

        def summed(scale, sums):
            pieces = [jnp.concatenate(split(mixed_ref[g, :, c * LANES : (c + 1) * LANES] * scale), 1) for c in range(tiles)]
            both = dot(jnp.concatenate(pieces, 0), sums)
            return [both[c * rows : (c + 1) * rows, :LANES] for c in range(tiles)], [both[c * rows : (c + 1) * rows, LANES:] for c in range(tiles)]

        east, all_east = summed(rising * gain, sums_east)
        west, all_west = summed(falling * gain, sums_west)
        carry = half * columns(state_ref[g * SUB : (g + 1) * SUB], levels)
        for c in range(tiles):
            east[c] = east[c] + carry
            carry = half * (half * (all_east[c] + carry))
        carry = half * columns(state_ref[MID + g * SUB : MID + (g + 1) * SUB], levels)
        for c in range(tiles - 1, -1, -1):
            west[c] = west[c] + carry
            carry = half * (half * (all_west[c] + carry))
        for c in range(tiles):
            filtered = falling * east[c] + rising * west[c]
            out_ref[:, :, g * tiles + c] = filtered.reshape(levels // 2, 2, SUB, LANES)


def filtered_blocks(where, decay, turned, edges, mixed):
    groups, rows, lons = mixed.shape
    levels, tiles = rows // SUB, lons // LANES
    return pl.pallas_call(
        filter_kernel,
        in_specs=[pl.BlockSpec(memory_space=pltpu.SMEM)] + [VMEM] * 4,
        out_specs=VMEM,
        out_shape=jax.ShapeDtypeStruct((levels // 2, 2, groups * tiles, SUB, LANES), jnp.float32),
        scratch_shapes=[pltpu.VMEM((LANES, LANES), jnp.float32)],
        compiler_params=pltpu.CompilerParams(vmem_limit_bytes=16 << 20),
        cost_estimate=pl.CostEstimate(flops=8 * 10**8, bytes_accessed=5 * 10**6, transcendentals=2 * 10**5),
        name="filter",
    )(where, decay, turned, edges, mixed)


def convolve_kernel(values_ref, kernel_ref, out_ref, high_ref, low_ref):
    sources, parts, lats, lons = out_ref.shape
    tiles = lons // LANES
    groups = lats // SUB
    for part in range(parts):
        for source in range(sources):
            rows = slice(source * lats, (source + 1) * lats)
            for c in range(tiles):
                values = jnp.concatenate([values_ref[source, part, g * tiles + c] for g in range(groups)], 0)
                cols = slice((part * tiles + c) * LANES, (part * tiles + c + 1) * LANES)
                high_ref[rows, cols], low_ref[rows, cols] = split(values)
    group = 4
    for j in range(0, sources, group):
        k_high, k_low = split(kernel_ref[j * lats : (j + group) * lats])
        result = dot3(k_high, k_low, high_ref[...], low_ref[...])
        for part in range(parts):
            out_ref[j : j + group, part] = result[:, part * lons : (part + 1) * lons].reshape(group, lats, lons)


def convolved(values, lat_kernel, lats, lons):
    sources = values.shape[0]
    nlat = sources * lats
    return pl.pallas_call(
        convolve_kernel,
        in_specs=[VMEM] * 2,
        out_specs=VMEM,
        out_shape=jax.ShapeDtypeStruct((sources, 2, lats, lons), jnp.float32),
        scratch_shapes=[
            pltpu.VMEM((nlat, 2 * lons), jnp.bfloat16),
            pltpu.VMEM((nlat, 2 * lons), jnp.bfloat16),
        ],
        compiler_params=pltpu.CompilerParams(vmem_limit_bytes=16 << 20),
        cost_estimate=pl.CostEstimate(flops=28 * 10**8, bytes_accessed=8 * 10**6, transcendentals=0),
        name="convolve",
    )(values, lat_kernel)


def on_device(field, vertical, rate, lat_kernel):
    ring = lax.axis_size("lon")
    levels, lats, lons = field.shape
    where = lax.axis_index("lon").reshape(1)

    def exchanged(v, axis):
        return lax.all_to_all(v, axis, 0, 0, tiled=True)

    mixed, edges, decay, turned = mixed_levels(ring, field, vertical, rate)
    where, edges = lax.optimization_barrier((where, edges))
    values = filtered_blocks(where, decay, turned, exchanged(edges, "lon"), mixed)
    out = convolved(exchanged(values, "lat"), lat_kernel, lats, lons)
    return exchanged(out, "lat").reshape(levels, lats, lons)


def solution(mesh):
    return jax.shard_map(
        on_device,
        mesh=mesh,
        in_specs=(P(None, "lat", "lon"), P(), P(None, "lat"), P()),
        out_specs=P(None, "lat", "lon"),
        check_vma=False,
    )
```

time: 96.8 us -> 94.9 us (0.980)
  Pallas kernels: 10.8 us -> 8.87 us
    pallas_call x1, Pallas kernels: 3.97 us -> 2.97 us  [convolved(): pl.pallas_call(convolve_kernel, in_specs=[VMEM] * 2, out_specs=VMEM, out_...]
where the time goes in v1:
time: 94.9 us; the launch traced here: 94.6 us
  blocking collectives  84.3 us (89%)
  Pallas kernels  8.87 us (9%)
  local copies, waits for them, and re-layouts  1.41 us (1%)
    all_to_all x3, blocking collectives, exchanged(): return lax.all_to_all(v, axis, 0, 0, tiled=True)  84.3 us
    pallas_call x1, Pallas kernels, mixed_levels(): pl.pallas_call(functools.partial(mix_kernel, 2 if groups % 2 == 0 else 1)...  3.74 us
    pallas_call x1, Pallas kernels, convolved(): pl.pallas_call(convolve_kernel, in_specs=[VMEM] * 2, out_specs=VMEM, out_...  2.97 us
    pallas_call x1, Pallas kernels, filtered_blocks(): pl.pallas_call(filter_kernel, in_specs=[pl.BlockSpec(memory_space=pltpu.S...  2.16 us

profile of v1, /device:TPU:1, one launch (start us, length us, event | category | flops | bytes accessed | tf_op | source)
XLA Modules:
  0.0 94.6 jit_solution(12995334414193318435)
XLA Ops:
  0.0 3.7 %mix.1 = (f32[6,256,384]{2,1,0:T(8,128)S(1)}, f32[8,32,128]{2,1,0:T(8,128)S(1)}, f32[32,128]{1,0:T(8,128)S(1)}, f32[2,128,128]{2,1,0:T(8,128)S(1)}) custom-call(f32[32,48,384]{2,1,0:T(8,128)} %field_hbm.1, f32[32,32]{1,0:T(8,128)} %vertical_hbm.1, f32[32,48]{1,0:T(8,128)} %rate_hbm.1), custom_call_target="tpu_custom_call" | custom-call | flops 800000000 | bytes 5000000 | tf_op jit(solution)/shard_map/mix/pallas_call | solution.py:112
  3.8 14.0 %all_to_all.15.edge_ref = f32[8,32,128]{2,1,0:T(8,128)S(1)} all-to-all(f32[8,32,128]{2,1,0:T(8,128)S(1)} %get-tuple-element.15), channel_id=1, replica_groups=mesh['lon'=8,'lat'=16] {'lon'}, dimensions={0} | all-to-all | bytes 262144 | tf_op jit(solution)/shard_map/all_to_all | solution.py:237
  17.8 2.2 %filter.1 = f32[16,2,18,8,128]{4,3,2,1,0:T(8,128)S(1)} custom-call(s32[1]{0:T(128)} %bitcast.place_ref, f32[32,128]{1,0:T(8,128)S(1)} %get-tuple-element.13.decay_ref, f32[2,128,128]{2,1,0:T(8,128)S(1)} %get-tuple-element.14.turned_ref, f32[8,32,128]{2,1,0:T(8,128)S(1)} %all_to_all.15.edge_ref, f32[6,256,384]{2,1,0:T(8,128)S(1)} %get-tuple-element.16.mixed_ref), custom_call_target="tpu_custom_call" | custom-call | flops 800000000 | bytes 5000000 | tf_op jit(solution)/shard_map/filter/pallas_call | solution.py:182
  19.9 0.0 copy-start
  20.0 37.1 %all_to_all.16.values_ref = f32[16,2,18,8,128]{4,3,2,1,0:T(8,128)S(1)} all-to-all(f32[16,2,18,8,128]{4,3,2,1,0:T(8,128)S(1)} %filter.1), channel_id=1, replica_groups=mesh['lon'=8,'lat'=16] {'lat'}, dimensions={0} | all-to-all | bytes 4718592 | tf_op jit(solution)/shard_map/all_to_all | solution.py:237
  57.1 0.0 copy-done
  57.1 3.0 %convolve.1 = f32[16,2,48,384]{3,2,1,0:T(8,128)S(1)} custom-call(f32[16,2,18,8,128]{4,3,2,1,0:T(8,128)S(1)} %all_to_all.16.values_ref, f32[768,768]{1,0:T(8,128)S(1)} %copy-done), custom_call_target="tpu_custom_call" | custom-call | flops 2800000000 | bytes 8000000 | tf_op jit(solution)/shard_map/convolve/pallas_call | solution.py:216
  60.1 33.1 %all_to_all.17 = f32[16,2,48,384]{3,2,1,0:T(8,128)S(1)} all-to-all(f32[16,2,48,384]{3,2,1,0:T(8,128)S(1)} %convolve.1), channel_id=1, replica_groups=mesh['lon'=8,'lat'=16] {'lat'}, dimensions={0} | all-to-all | bytes 4718592 | tf_op jit(solution)/shard_map/all_to_all | solution.py:237
  93.2 1.4 %copy.6 = f32[32,48,384]{2,1,0:T(8,128)} copy(f32[32,48,384]{2,1,0:T(8,128)S(1)} %bitcast.2) | data formatting | bytes 4718592
Async XLA Ops:
  19.9 37.1 %copy-start = (f32[768,768]{1,0:T(8,128)S(1)}, f32[768,768]{1,0:T(8,128)}, u32[]{:S(2)}) copy-start(f32[768,768]{1,0:T(8,128)} %kernel_ref.1) | copy-start | bytes 7077892

commit v2 on v1

--- a/solution.py
+++ b/solution.py
@@ -110,7 +110,7 @@
     levels, lats, lons = field.shape
     groups, rows = lats // SUB, levels * SUB
     return pl.pallas_call(
-        functools.partial(mix_kernel, 2 if groups % 2 == 0 else 1),
+        functools.partial(mix_kernel, groups),
         in_specs=[HBM] * 3,
         out_specs=[VMEM] * 4,
         out_shape=[
@@ -133,7 +133,7 @@
     )(*[pltpu.with_memory_space_constraint(v, pltpu.HBM) for v in (field, vertical, rate)])
 
 
-def filter_kernel(place_ref, decay_ref, turned_ref, edge_ref, mixed_ref, out_ref, state_ref):
+def filter_kernel(batch, place_ref, decay_ref, turned_ref, edge_ref, mixed_ref, out_ref, state_ref):
     groups, rows, lons = mixed_ref.shape
     ring, levels, _ = edge_ref.shape
     tiles = lons // LANES
@@ -150,37 +150,40 @@
     sums_east = ((source <= target) | (target >= LANES)).astype(jnp.bfloat16)
     sums_west = ((source > target) | (target >= LANES)).astype(jnp.bfloat16)
     offset = (iota((rows, LANES), 1) - MID).astype(jnp.float32)
-    for g in range(groups):
-        here = slice(g * SUB, (g + 1) * SUB)
-        log_decay, gain = columns(turned_ref[0, here], levels), columns(turned_ref[1, here], levels)
-        falling, rising = jnp.exp(offset * log_decay), jnp.exp(-offset * log_decay)
-        half = jnp.exp(MID * log_decay)
-
-        def summed(scale, sums):
-            pieces = [jnp.concatenate(split(mixed_ref[g, :, c * LANES : (c + 1) * LANES] * scale), 1) for c in range(tiles)]
-            both = dot(jnp.concatenate(pieces, 0), sums)
-            return [both[c * rows : (c + 1) * rows, :LANES] for c in range(tiles)], [both[c * rows : (c + 1) * rows, LANES:] for c in range(tiles)]
-
-        east, all_east = summed(rising * gain, sums_east)
-        west, all_west = summed(falling * gain, sums_west)
-        carry = half * columns(state_ref[g * SUB : (g + 1) * SUB], levels)
-        for c in range(tiles):
-            east[c] = east[c] + carry
-            carry = half * (half * (all_east[c] + carry))
-        carry = half * columns(state_ref[MID + g * SUB : MID + (g + 1) * SUB], levels)
-        for c in range(tiles - 1, -1, -1):
-            west[c] = west[c] + carry
-            carry = half * (half * (all_west[c] + carry))
-        for c in range(tiles):
-            filtered = falling * east[c] + rising * west[c]
-            out_ref[:, :, g * tiles + c] = filtered.reshape(levels // 2, 2, SUB, LANES)
+    for first_group in range(0, groups, batch):
+        batched = range(first_group, first_group + batch)
+        falling, rising, half, from_east, from_west = [], [], [], [], []
+        for g in batched:
+            here = slice(g * SUB, (g + 1) * SUB)
+            log_decay, gain = columns(turned_ref[0, here], levels), columns(turned_ref[1, here], levels)
+            falling.append(jnp.exp(offset * log_decay))
+            rising.append(jnp.exp(-offset * log_decay))
+            half.append(jnp.exp(MID * log_decay))
+            for scale, pieces in ((rising[-1] * gain, from_east), (falling[-1] * gain, from_west)):
+                pieces += [jnp.concatenate(split(mixed_ref[g, :, c * LANES : (c + 1) * LANES] * scale), 1) for c in range(tiles)]
+        sums = [dot(jnp.concatenate(pieces, 0), table) for pieces, table in ((from_east, sums_east), (from_west, sums_west))]
+        for at, g in enumerate(batched):
+            east, west = ([s[(at * tiles + c) * rows : (at * tiles + c + 1) * rows] for c in range(tiles)] for s in sums)
+            carry = half[at] * columns(state_ref[g * SUB : (g + 1) * SUB], levels)
+            for c in range(tiles):
+                onward = half[at] * (half[at] * (east[c][:, LANES:] + carry))
+                east[c] = east[c][:, :LANES] + carry
+                carry = onward
+            carry = half[at] * columns(state_ref[MID + g * SUB : MID + (g + 1) * SUB], levels)
+            for c in range(tiles - 1, -1, -1):
+                onward = half[at] * (half[at] * (west[c][:, LANES:] + carry))
+                west[c] = west[c][:, :LANES] + carry
+                carry = onward
+            for c in range(tiles):
+                filtered = falling[at] * east[c] + rising[at] * west[c]
+                out_ref[:, :, g * tiles + c] = filtered.reshape(levels // 2, 2, SUB, LANES)
 
 
 def filtered_blocks(where, decay, turned, edges, mixed):
     groups, rows, lons = mixed.shape
     levels, tiles = rows // SUB, lons // LANES
     return pl.pallas_call(
-        filter_kernel,
+        functools.partial(filter_kernel, groups),
         in_specs=[pl.BlockSpec(memory_space=pltpu.SMEM)] + [VMEM] * 4,
         out_specs=VMEM,
         out_shape=jax.ShapeDtypeStruct((levels // 2, 2, groups * tiles, SUB, LANES), jnp.float32),

time: 94.9 us -> 94.5 us (level)
  no operation moved by 1% of the time
where the time goes in v2:
time: 94.5 us; the launch traced here: 94.2 us
  blocking collectives  84.3 us (89%)
  Pallas kernels  8.49 us (9%)
  local copies, waits for them, and re-layouts  1.41 us (1%)
    all_to_all x3, blocking collectives, exchanged(): return lax.all_to_all(v, axis, 0, 0, tiled=True)  84.3 us
    pallas_call x1, Pallas kernels, mixed_levels(): pl.pallas_call(functools.partial(mix_kernel, groups), in_specs=[HBM] * 3,...  3.45 us
    pallas_call x1, Pallas kernels, convolved(): pl.pallas_call(convolve_kernel, in_specs=[VMEM] * 2, out_specs=VMEM, out_...  2.96 us
    pallas_call x1, Pallas kernels, filtered_blocks(): pl.pallas_call(functools.partial(filter_kernel, groups), in_specs=[pl.Blo...  2.08 us

profile of v2, /device:TPU:1, one launch (start us, length us, event | category | flops | bytes accessed | tf_op | source)
XLA Modules:
  0.0 94.2 jit_solution(924854203531294892)
XLA Ops:
  0.0 3.5 %mix.1 = (f32[6,256,384]{2,1,0:T(8,128)S(1)}, f32[8,32,128]{2,1,0:T(8,128)S(1)}, f32[32,128]{1,0:T(8,128)S(1)}, f32[2,128,128]{2,1,0:T(8,128)S(1)}) custom-call(f32[32,48,384]{2,1,0:T(8,128)} %field_hbm.1, f32[32,32]{1,0:T(8,128)} %vertical_hbm.1, f32[32,48]{1,0:T(8,128)} %rate_hbm.1), custom_call_target="tpu_custom_call" | custom-call | flops 800000000 | bytes 5000000 | tf_op jit(solution)/shard_map/mix/pallas_call | solution.py:112
  3.5 14.0 %all_to_all.15.edge_ref = f32[8,32,128]{2,1,0:T(8,128)S(1)} all-to-all(f32[8,32,128]{2,1,0:T(8,128)S(1)} %get-tuple-element.15), channel_id=1, replica_groups=mesh['lon'=8,'lat'=16] {'lon'}, dimensions={0} | all-to-all | bytes 262144 | tf_op jit(solution)/shard_map/all_to_all | solution.py:240
  17.5 2.1 %filter.1 = f32[16,2,18,8,128]{4,3,2,1,0:T(8,128)S(1)} custom-call(s32[1]{0:T(128)} %bitcast.place_ref, f32[32,128]{1,0:T(8,128)S(1)} %get-tuple-element.13.decay_ref, f32[2,128,128]{2,1,0:T(8,128)S(1)} %get-tuple-element.14.turned_ref, f32[8,32,128]{2,1,0:T(8,128)S(1)} %all_to_all.15.edge_ref, f32[6,256,384]{2,1,0:T(8,128)S(1)} %get-tuple-element.16.mixed_ref), custom_call_target="tpu_custom_call" | custom-call | flops 800000000 | bytes 5000000 | tf_op jit(solution)/shard_map/filter/pallas_call | solution.py:185
  19.6 0.0 copy-start
  19.6 37.1 %all_to_all.16.values_ref = f32[16,2,18,8,128]{4,3,2,1,0:T(8,128)S(1)} all-to-all(f32[16,2,18,8,128]{4,3,2,1,0:T(8,128)S(1)} %filter.1), channel_id=1, replica_groups=mesh['lon'=8,'lat'=16] {'lat'}, dimensions={0} | all-to-all | bytes 4718592 | tf_op jit(solution)/shard_map/all_to_all | solution.py:240
  56.7 0.0 copy-done
  56.7 3.0 %convolve.1 = f32[16,2,48,384]{3,2,1,0:T(8,128)S(1)} custom-call(f32[16,2,18,8,128]{4,3,2,1,0:T(8,128)S(1)} %all_to_all.16.values_ref, f32[768,768]{1,0:T(8,128)S(1)} %copy-done), custom_call_target="tpu_custom_call" | custom-call | flops 2800000000 | bytes 8000000 | tf_op jit(solution)/shard_map/convolve/pallas_call | solution.py:219
  59.7 33.1 %all_to_all.17 = f32[16,2,48,384]{3,2,1,0:T(8,128)S(1)} all-to-all(f32[16,2,48,384]{3,2,1,0:T(8,128)S(1)} %convolve.1), channel_id=1, replica_groups=mesh['lon'=8,'lat'=16] {'lat'}, dimensions={0} | all-to-all | bytes 4718592 | tf_op jit(solution)/shard_map/all_to_all | solution.py:240
  92.8 1.4 %copy.6 = f32[32,48,384]{2,1,0:T(8,128)} copy(f32[32,48,384]{2,1,0:T(8,128)S(1)} %bitcast.2) | data formatting | bytes 4718592
Async XLA Ops:
  19.6 37.1 %copy-start = (f32[768,768]{1,0:T(8,128)S(1)}, f32[768,768]{1,0:T(8,128)}, u32[]{:S(2)}) copy-start(f32[768,768]{1,0:T(8,128)} %kernel_ref.1) | copy-start | bytes 7077892

commit v3 on v2

--- a/solution.py
+++ b/solution.py
@@ -74,6 +74,7 @@
 
     lane = iota((rows, LANES), 1).astype(jnp.float32)
     narrow = iota((SUB, LANES), 1)
+    weighted = []
     for first_group in range(0, groups, batch):
         batched = range(first_group, first_group + batch)
         for g in batched:
@@ -93,12 +94,14 @@
                 first = first * hop + value[tiles - 1 - c]
             last = last * jnp.exp((LANES - lane) * log_decay)
             first = first * jnp.exp(lane * log_decay)
-            for weighted, base in ((last, 0), (first, MID)):
-                total = dot(jnp.concatenate(split(weighted), 1), ones)
-                edges = jnp.zeros((SUB, LANES), jnp.float32)
-                for k in range(levels):
-                    edges = jnp.where(narrow == k, total[k * SUB : (k + 1) * SUB], edges)
-                edges_ref[base + g * SUB : base + (g + 1) * SUB, :] = edges * turned_ref[1, here]
+            weighted += [(last, g * SUB, here), (first, MID + g * SUB, here)]
+    totals = dot(jnp.concatenate([jnp.concatenate(split(v), 1) for v, _, _ in weighted], 0), ones)
+    for i, (_, base, here) in enumerate(weighted):
+        edges = jnp.zeros((SUB, LANES), jnp.float32)
+        for k in range(levels):
+            at = i * rows + k * SUB
+            edges = jnp.where(narrow == k, totals[at : at + SUB], edges)
+        edges_ref[base : base + SUB, :] = edges * turned_ref[1, here]
     edge_ref[...] = jnp.broadcast_to(edges_ref[...].T[None, :levels], edge_ref.shape)
 
 
@@ -198,17 +201,15 @@
     sources, parts, lats, lons = out_ref.shape
     tiles = lons // LANES
     groups = lats // SUB
+    strips = []
     for part in range(parts):
-        for source in range(sources):
-            rows = slice(source * lats, (source + 1) * lats)
-            for c in range(tiles):
-                values = jnp.concatenate([values_ref[source, part, g * tiles + c] for g in range(groups)], 0)
-                cols = slice((part * tiles + c) * LANES, (part * tiles + c + 1) * LANES)
-                high_ref[rows, cols], low_ref[rows, cols] = split(values)
+        for c in range(tiles):
+            strips.append(jnp.concatenate([values_ref[source, part, g * tiles + c] for source in range(sources) for g in range(groups)], 0))
+    f_high, f_low = split(jnp.concatenate(strips, 1))
     group = 4
     for j in range(0, sources, group):
         k_high, k_low = split(kernel_ref[j * lats : (j + group) * lats])
-        result = dot3(k_high, k_low, high_ref[...], low_ref[...])
+        result = dot3(k_high, k_low, f_high, f_low)
         for part in range(parts):
             out_ref[j : j + group, part] = result[:, part * lons : (part + 1) * lons].reshape(group, lats, lons)
 

time: 94.5 us -> 94.4 us (level)
  no operation moved by 1% of the time
where the time goes in v3:
time: 94.4 us; the launch traced here: 94.1 us
  blocking collectives  84.3 us (89%)
  Pallas kernels  8.38 us (9%)
  local copies, waits for them, and re-layouts  1.41 us (1%)
    all_to_all x3, blocking collectives, exchanged(): return lax.all_to_all(v, axis, 0, 0, tiled=True)  84.3 us
    pallas_call x1, Pallas kernels, mixed_levels(): pl.pallas_call(functools.partial(mix_kernel, groups), in_specs=[HBM] * 3,...  3.38 us
    pallas_call x1, Pallas kernels, convolved(): pl.pallas_call(convolve_kernel, in_specs=[VMEM] * 2, out_specs=VMEM, out_...  2.92 us
    pallas_call x1, Pallas kernels, filtered_blocks(): pl.pallas_call(functools.partial(filter_kernel, groups), in_specs=[pl.Blo...  2.08 us

profile of v3, /device:TPU:1, one launch (start us, length us, event | category | flops | bytes accessed | tf_op | source)
XLA Modules:
  0.0 94.1 jit_solution(10684680283160139995)
XLA Ops:
  0.0 3.4 %mix.1 = (f32[6,256,384]{2,1,0:T(8,128)S(1)}, f32[8,32,128]{2,1,0:T(8,128)S(1)}, f32[32,128]{1,0:T(8,128)S(1)}, f32[2,128,128]{2,1,0:T(8,128)S(1)}) custom-call(f32[32,48,384]{2,1,0:T(8,128)} %field_hbm.1, f32[32,32]{1,0:T(8,128)} %vertical_hbm.1, f32[32,48]{1,0:T(8,128)} %rate_hbm.1), custom_call_target="tpu_custom_call" | custom-call | flops 800000000 | bytes 5000000 | tf_op jit(solution)/shard_map/mix/pallas_call | solution.py:115
  3.4 14.0 %all_to_all.15.edge_ref = f32[8,32,128]{2,1,0:T(8,128)S(1)} all-to-all(f32[8,32,128]{2,1,0:T(8,128)S(1)} %get-tuple-element.15), channel_id=1, replica_groups=mesh['lon'=8,'lat'=16] {'lon'}, dimensions={0} | all-to-all | bytes 262144 | tf_op jit(solution)/shard_map/all_to_all | solution.py:241
  17.4 2.1 %filter.1 = f32[16,2,18,8,128]{4,3,2,1,0:T(8,128)S(1)} custom-call(s32[1]{0:T(128)} %bitcast.place_ref, f32[32,128]{1,0:T(8,128)S(1)} %get-tuple-element.13.decay_ref, f32[2,128,128]{2,1,0:T(8,128)S(1)} %get-tuple-element.14.turned_ref, f32[8,32,128]{2,1,0:T(8,128)S(1)} %all_to_all.15.edge_ref, f32[6,256,384]{2,1,0:T(8,128)S(1)} %get-tuple-element.16.mixed_ref), custom_call_target="tpu_custom_call" | custom-call | flops 800000000 | bytes 5000000 | tf_op jit(solution)/shard_map/filter/pallas_call | solution.py:188
  19.5 0.0 copy-start
  19.5 37.1 %all_to_all.16.values_ref = f32[16,2,18,8,128]{4,3,2,1,0:T(8,128)S(1)} all-to-all(f32[16,2,18,8,128]{4,3,2,1,0:T(8,128)S(1)} %filter.1), channel_id=1, replica_groups=mesh['lon'=8,'lat'=16] {'lat'}, dimensions={0} | all-to-all | bytes 4718592 | tf_op jit(solution)/shard_map/all_to_all | solution.py:241
  56.6 0.0 copy-done
  56.6 2.9 %convolve.1 = f32[16,2,48,384]{3,2,1,0:T(8,128)S(1)} custom-call(f32[16,2,18,8,128]{4,3,2,1,0:T(8,128)S(1)} %all_to_all.16.values_ref, f32[768,768]{1,0:T(8,128)S(1)} %copy-done), custom_call_target="tpu_custom_call" | custom-call | flops 2800000000 | bytes 8000000 | tf_op jit(solution)/shard_map/convolve/pallas_call | solution.py:220
  59.6 33.1 %all_to_all.17 = f32[16,2,48,384]{3,2,1,0:T(8,128)S(1)} all-to-all(f32[16,2,48,384]{3,2,1,0:T(8,128)S(1)} %convolve.1), channel_id=1, replica_groups=mesh['lon'=8,'lat'=16] {'lat'}, dimensions={0} | all-to-all | bytes 4718592 | tf_op jit(solution)/shard_map/all_to_all | solution.py:241
  92.7 1.4 %copy.6 = f32[32,48,384]{2,1,0:T(8,128)} copy(f32[32,48,384]{2,1,0:T(8,128)S(1)} %bitcast.2) | data formatting | bytes 4718592
Async XLA Ops:
  19.5 37.1 %copy-start = (f32[768,768]{1,0:T(8,128)S(1)}, f32[768,768]{1,0:T(8,128)}, u32[]{:S(2)}) copy-start(f32[768,768]{1,0:T(8,128)} %kernel_ref.1) | copy-start | bytes 7077892

commit v4 on v3

--- a/solution.py
+++ b/solution.py
@@ -39,7 +39,7 @@
     return jnp.concatenate([jnp.broadcast_to(tile[:, k : k + 1], (SUB, LANES)) for k in range(levels)], 0)
 
 
-def mix_kernel(batch, field_hbm, vertical_hbm, rate_hbm, mixed_ref, edge_ref, decay_ref, turned_ref, field_ref, vertical_ref, rate_ref, matrix_ref, edges_ref, sems):
+def mix_kernel(batch, field_hbm, vertical_hbm, rate_hbm, mixed_ref, edge_ref, decay_ref, turned_ref, sums_ref, field_ref, vertical_ref, rate_ref, matrix_ref, edges_ref, sems):
     groups, rows, lons = mixed_ref.shape
     levels = rows // SUB
     lats = groups * SUB
@@ -57,6 +57,9 @@
     across = (iota((levels, rows), 1) // SUB == iota((levels, rows), 0)).astype(jnp.bfloat16)
     same = iota((rows, rows), 0) % SUB == iota((rows, rows), 1) % SUB
     ones = jnp.ones((2 * LANES, LANES), jnp.bfloat16)
+    source, target = iota((2 * LANES, 2 * LANES), 0) % LANES, iota((2 * LANES, 2 * LANES), 1)
+    sums_ref[0] = ((source <= target) | (target >= LANES)).astype(jnp.bfloat16)
+    sums_ref[1] = ((source > target) | (target >= LANES)).astype(jnp.bfloat16)
     edges_ref[...] = jnp.zeros_like(edges_ref)
     small[0].wait()
     filled = jnp.full((levels, MID - lats), 0.5, jnp.float32)
@@ -115,12 +118,13 @@
     return pl.pallas_call(
         functools.partial(mix_kernel, groups),
         in_specs=[HBM] * 3,
-        out_specs=[VMEM] * 4,
+        out_specs=[VMEM] * 5,
         out_shape=[
             jax.ShapeDtypeStruct((groups, rows, lons), jnp.float32),
             jax.ShapeDtypeStruct((ring, levels, LANES), jnp.float32),
             jax.ShapeDtypeStruct((levels, LANES), jnp.float32),
             jax.ShapeDtypeStruct((2, LANES, LANES), jnp.float32),
+            jax.ShapeDtypeStruct((2, 2 * LANES, 2 * LANES), jnp.bfloat16),
         ],
         scratch_shapes=[
             pltpu.VMEM((groups, levels, SUB, lons), jnp.float32),
@@ -136,7 +140,7 @@
     )(*[pltpu.with_memory_space_constraint(v, pltpu.HBM) for v in (field, vertical, rate)])
 
 
-def filter_kernel(batch, place_ref, decay_ref, turned_ref, edge_ref, mixed_ref, out_ref, state_ref):
+def filter_kernel(batch, place_ref, decay_ref, turned_ref, sums_ref, edge_ref, mixed_ref, out_ref, state_ref):
     groups, rows, lons = mixed_ref.shape
     ring, levels, _ = edge_ref.shape
     tiles = lons // LANES
@@ -149,9 +153,7 @@
         total = total + edge_ref[device] * jnp.exp(blocks * (lons * log_decay))
     total = total / (1.0 - jnp.exp((ring * lons) * log_decay))
     state_ref[...] = jnp.concatenate([total, jnp.zeros((LANES - levels, LANES), jnp.float32)], 0).T
-    source, target = iota((2 * LANES, 2 * LANES), 0) % LANES, iota((2 * LANES, 2 * LANES), 1)
-    sums_east = ((source <= target) | (target >= LANES)).astype(jnp.bfloat16)
-    sums_west = ((source > target) | (target >= LANES)).astype(jnp.bfloat16)
+    sums_east, sums_west = sums_ref[0], sums_ref[1]
     offset = (iota((rows, LANES), 1) - MID).astype(jnp.float32)
     for first_group in range(0, groups, batch):
         batched = range(first_group, first_group + batch)
@@ -182,19 +184,19 @@
                 out_ref[:, :, g * tiles + c] = filtered.reshape(levels // 2, 2, SUB, LANES)
 
 
-def filtered_blocks(where, decay, turned, edges, mixed):
+def filtered_blocks(where, decay, turned, sums, edges, mixed):
     groups, rows, lons = mixed.shape
     levels, tiles = rows // SUB, lons // LANES
     return pl.pallas_call(
         functools.partial(filter_kernel, groups),
-        in_specs=[pl.BlockSpec(memory_space=pltpu.SMEM)] + [VMEM] * 4,
+        in_specs=[pl.BlockSpec(memory_space=pltpu.SMEM)] + [VMEM] * 5,
         out_specs=VMEM,
         out_shape=jax.ShapeDtypeStruct((levels // 2, 2, groups * tiles, SUB, LANES), jnp.float32),
         scratch_shapes=[pltpu.VMEM((LANES, LANES), jnp.float32)],
         compiler_params=pltpu.CompilerParams(vmem_limit_bytes=16 << 20),
         cost_estimate=pl.CostEstimate(flops=8 * 10**8, bytes_accessed=5 * 10**6, transcendentals=2 * 10**5),
         name="filter",
-    )(where, decay, turned, edges, mixed)
+    )(where, decay, turned, sums, edges, mixed)
 
 
 def convolve_kernel(values_ref, kernel_ref, out_ref, high_ref, low_ref):
@@ -240,9 +242,9 @@
     def exchanged(v, axis):
         return lax.all_to_all(v, axis, 0, 0, tiled=True)
 
-    mixed, edges, decay, turned = mixed_levels(ring, field, vertical, rate)
+    mixed, edges, decay, turned, sums = mixed_levels(ring, field, vertical, rate)
     where, edges = lax.optimization_barrier((where, edges))
-    values = filtered_blocks(where, decay, turned, exchanged(edges, "lon"), mixed)
+    values = filtered_blocks(where, decay, turned, sums, exchanged(edges, "lon"), mixed)
     out = convolved(exchanged(values, "lat"), lat_kernel, lats, lons)
     return exchanged(out, "lat").reshape(levels, lats, lons)
 

time: 94.4 us -> 94.4 us (level)
  no operation moved by 1% of the time
where the time goes in v4:
time: 94.4 us; the launch traced here: 94.1 us
  blocking collectives  84.3 us (89%)
  Pallas kernels  8.38 us (9%)
  local copies, waits for them, and re-layouts  1.41 us (1%)
    all_to_all x3, blocking collectives, exchanged(): return lax.all_to_all(v, axis, 0, 0, tiled=True)  84.3 us
    pallas_call x1, Pallas kernels, mixed_levels(): pl.pallas_call(functools.partial(mix_kernel, groups), in_specs=[HBM] * 3,...  3.39 us
    pallas_call x1, Pallas kernels, convolved(): pl.pallas_call(convolve_kernel, in_specs=[VMEM] * 2, out_specs=VMEM, out_...  2.91 us
    pallas_call x1, Pallas kernels, filtered_blocks(): pl.pallas_call(functools.partial(filter_kernel, groups), in_specs=[pl.Blo...  2.08 us

profile of v4, /device:TPU:1, one launch (start us, length us, event | category | flops | bytes accessed | tf_op | source)
XLA Modules:
  0.0 94.1 jit_solution(11187537929967530832)
XLA Ops:
  0.0 3.4 %mix.1 = (f32[6,256,384]{2,1,0:T(8,128)S(1)}, f32[8,32,128]{2,1,0:T(8,128)S(1)}, f32[32,128]{1,0:T(8,128)S(1)}, f32[2,128,128]{2,1,0:T(8,128)S(1)}, bf16[2,256,256]{2,1,0:T(8,128)(2,1)S(1)}) custom-call(f32[32,48,384]{2,1,0:T(8,128)} %field_hbm.1, f32[32,32]{1,0:T(8,128)} %vertical_hbm.1, f32[32,48]{1,0:T(8,128)} %rate_hbm.1), custom_call_target="tpu_custom_call" | custom-call | flops 800000000 | bytes 5000000 | tf_op jit(solution)/shard_map/mix/pallas_call | solution.py:118
  3.4 14.0 %all_to_all.15.edge_ref = f32[8,32,128]{2,1,0:T(8,128)S(1)} all-to-all(f32[8,32,128]{2,1,0:T(8,128)S(1)} %get-tuple-element.17), channel_id=1, replica_groups=mesh['lon'=8,'lat'=16] {'lon'}, dimensions={0} | all-to-all | bytes 262144 | tf_op jit(solution)/shard_map/all_to_all | solution.py:243
  17.4 2.1 %filter.1 = f32[16,2,18,8,128]{4,3,2,1,0:T(8,128)S(1)} custom-call(s32[1]{0:T(128)} %bitcast.place_ref, f32[32,128]{1,0:T(8,128)S(1)} %get-tuple-element.14.decay_ref, f32[2,128,128]{2,1,0:T(8,128)S(1)} %get-tuple-element.15.turned_ref, bf16[2,256,256]{2,1,0:T(8,128)(2,1)S(1)} %get-tuple-element.16.sums_ref, f32[8,32,128]{2,1,0:T(8,128)S(1)} %all_to_all.15.edge_ref, ...), custom_call_target="tpu_custom_call" | custom-call | flops 800000000 | bytes 5000000 | tf_op jit(solution)/shard_map/filter/pallas_call | solution.py:190
  19.5 0.0 copy-start
  19.5 37.1 %all_to_all.16.values_ref = f32[16,2,18,8,128]{4,3,2,1,0:T(8,128)S(1)} all-to-all(f32[16,2,18,8,128]{4,3,2,1,0:T(8,128)S(1)} %filter.1), channel_id=1, replica_groups=mesh['lon'=8,'lat'=16] {'lat'}, dimensions={0} | all-to-all | bytes 4718592 | tf_op jit(solution)/shard_map/all_to_all | solution.py:243
  56.6 0.0 copy-done
  56.6 2.9 %convolve.1 = f32[16,2,48,384]{3,2,1,0:T(8,128)S(1)} custom-call(f32[16,2,18,8,128]{4,3,2,1,0:T(8,128)S(1)} %all_to_all.16.values_ref, f32[768,768]{1,0:T(8,128)S(1)} %copy-done), custom_call_target="tpu_custom_call" | custom-call | flops 2800000000 | bytes 8000000 | tf_op jit(solution)/shard_map/convolve/pallas_call | solution.py:222
  59.6 33.1 %all_to_all.17 = f32[16,2,48,384]{3,2,1,0:T(8,128)S(1)} all-to-all(f32[16,2,48,384]{3,2,1,0:T(8,128)S(1)} %convolve.1), channel_id=1, replica_groups=mesh['lon'=8,'lat'=16] {'lat'}, dimensions={0} | all-to-all | bytes 4718592 | tf_op jit(solution)/shard_map/all_to_all | solution.py:243
  92.7 1.4 %copy.6 = f32[32,48,384]{2,1,0:T(8,128)} copy(f32[32,48,384]{2,1,0:T(8,128)S(1)} %bitcast.2) | data formatting | bytes 4718592
Async XLA Ops:
  19.5 37.1 %copy-start = (f32[768,768]{1,0:T(8,128)S(1)}, f32[768,768]{1,0:T(8,128)}, u32[]{:S(2)}) copy-start(f32[768,768]{1,0:T(8,128)} %kernel_ref.1) | copy-start | bytes 7077892
